TPU v7x, 128 devices: a whole 4x4x4 slice. The times are simulated.
128 devices in a mesh: layer: 32 (over x_hi, y, z), dir: 4 (over x_lo, core).
Axes of the slice: x: 4 (x_hi: 2, x_lo: 2; x = x_hi * 2 + x_lo), y: 4, z: 4, core: 2. Of those that a mesh axis runs over, the one named last changes fastest.
Arguments:
- screens: bfloat16 [3, 2048, 16384], P(None, 'dir', 'layer'), may hold values from -6 to 6
- amplitude: float32 [1024, 1280], P('layer'), may hold values from 0.5 to 2
- wind: int32 [3, 2], replicated, may hold values from -8 to 8, as said below
- offsets: int32 [4, 3, 2], replicated, may hold values from 0 to 16383, as said below
- ratio: int32 [4, 3, 2], replicated, may hold values from 64 to 192, as said below
Outputs:
- new_screens: bfloat16 [3, 2048, 16384], P(None, 'dir', 'layer')
- spots: float32 [4, 2048, 2560], P('dir', 'layer')
Inputs may be any that keep to these rules, and one draw needn't show every extreme that they name: wind[l, 0] is layer l's row shift and wind[l, 1] its column shift; no shift is zero; one layer has column shift +8 and a row shift above zero, another has column shift -8 and a row shift below zero. offsets[d, l, 0] is a screen row below 2048, offsets[d, l, 1] a screen column below 16384. ratio[d, l] = (num, den) with 64 <= den <= 128 and den <= num <= den + den // 2; some entry is (192, 128) and another (64, 64).
All inputs are finite; a program needn't handle non-finite values.
Results may differ from a plain program's by a relative error of at most 0.009.
Values may be sent and summed in bfloat16 or wider, within the bound.
A program may use at most 64 MiB of HBM per device.

v0:
```python
import jax
import jax.numpy as jnp
from jax import lax
from jax.sharding import PartitionSpec as P

SUB_PIX = 16
SPOT_PIX = 32
WIND_MAX = 8


def with_halo(shard, sides, width):
    for axis, dim in sides:
        peers, length = (lax.axis_size(axis), shard.shape[dim])
        up = [(i, (i + 1) % peers) for i in range(peers)]
        down = [(j, i) for i, j in up]
        last = lax.slice_in_dim(shard, length - width, length, axis=dim)
        initial = lax.slice_in_dim(shard, 0, width, axis=dim)
        before = lax.ppermute(last, axis, up)
        after = lax.ppermute(initial, axis, down)
        shard = jnp.concatenate([before, shard, after], axis=dim)
    return shard


def spans(anchor, stretch_num, stretch_den, count, length):
    pixel = jnp.arange(count, dtype=jnp.int32)
    stretched = pixel * stretch_num
    base = (anchor + stretched // stretch_den) % length
    upper = (base + 1) % length
    fraction = (stretched % stretch_den).astype(jnp.float32) / stretch_den.astype(jnp.float32)
    return (base, upper, (1.0 - fraction).astype(jnp.bfloat16), fraction.astype(jnp.bfloat16))


def weights_rows(anchor, stretch_num, stretch_den, count, length, width):
    base, upper, low_weight, high_weight = spans(anchor, stretch_num, stretch_den, count, length)
    index = jnp.arange(width, dtype=jnp.int32)
    matrix = jnp.where(
        index[None, :] == base[:, None], low_weight[:, None], jnp.zeros((), jnp.bfloat16)
    )
    return jnp.where(index[None, :] == upper[:, None], high_weight[:, None], matrix)


def weights_cols(anchor, stretch_num, stretch_den, count, length, start, width):
    base, upper, low_weight, high_weight = spans(anchor, stretch_num, stretch_den, count, length)
    index = start + jnp.arange(width, dtype=jnp.int32)
    matrix = jnp.where(
        index[:, None] == base[None, :], low_weight[None, :], jnp.zeros((), jnp.bfloat16)
    )
    return jnp.where(index[:, None] == upper[None, :], high_weight[None, :], matrix)


def dft_tables():
    freq = jnp.arange(SPOT_PIX, dtype=jnp.int32)[:, None] - SPOT_PIX // 2
    pixel = jnp.arange(SUB_PIX, dtype=jnp.int32)[None, :]
    turns = freq * pixel % SPOT_PIX
    angle = turns.astype(jnp.float32) * (2.0 * jnp.pi / SPOT_PIX)
    return (jnp.cos(angle), -jnp.sin(angle))


def imaging(phase, amplitude):
    rows, cols = phase.shape
    sub_rows = rows // SUB_PIX
    sub_cols = cols // SUB_PIX
    real = (amplitude * jnp.cos(phase)).reshape(sub_rows, SUB_PIX, sub_cols, SUB_PIX)
    imag = (amplitude * jnp.sin(phase)).reshape(sub_rows, SUB_PIX, sub_cols, SUB_PIX)
    cos_table, sin_table = dft_tables()
    highest = lax.Precision.HIGHEST
    half_real = jnp.einsum("aibj,kj->aibk", real, cos_table, precision=highest) - jnp.einsum(
        "aibj,kj->aibk", imag, sin_table, precision=highest
    )
    half_imag = jnp.einsum("aibj,kj->aibk", real, sin_table, precision=highest) + jnp.einsum(
        "aibj,kj->aibk", imag, cos_table, precision=highest
    )
    full_real = jnp.einsum("ki,aibl->akbl", cos_table, half_real, precision=highest) - jnp.einsum(
        "ki,aibl->akbl", sin_table, half_imag, precision=highest
    )
    full_imag = jnp.einsum("ki,aibl->akbl", cos_table, half_imag, precision=highest) + jnp.einsum(
        "ki,aibl->akbl", sin_table, half_real, precision=highest
    )
    intensity = full_real * full_real + full_imag * full_imag
    totals = jnp.sum(intensity, axis=(1, 3), keepdims=True)
    normed = intensity * float(SPOT_PIX * SPOT_PIX) / totals
    return normed.reshape(sub_rows * SPOT_PIX, sub_cols * SPOT_PIX)


def per_device(screens, amplitude, wind, offsets, ratio):
    layers, rows_dev, cols_dev = screens.shape
    n_layer = lax.axis_size("layer")
    n_dir = lax.axis_size("dir")
    screen_rows = rows_dev * n_dir
    screen_cols = cols_dev * n_layer
    pupil_rows = amplitude.shape[0] * n_layer
    pupil_cols = amplitude.shape[1]
    direction = lax.axis_index("dir")
    column_start = lax.axis_index("layer") * cols_dev
    widened = with_halo(screens, (("layer", 2), ("dir", 1)), WIND_MAX)
    moved = []
    for level in range(layers):
        corner = (jnp.int32(WIND_MAX) - wind[level, 0], jnp.int32(WIND_MAX) - wind[level, 1])
        moved.append(lax.dynamic_slice(widened[level], corner, (rows_dev, cols_dev)))
    new_screens = jnp.stack(moved)
    piece = lax.all_gather(new_screens, "dir", axis=1, tiled=True)
    sums = []
    for add_level in range(layers):
        weights = weights_rows(
            offsets[direction, add_level, 0],
            ratio[direction, add_level, 0],
            ratio[direction, add_level, 1],
            pupil_rows,
            screen_rows,
            piece.shape[1],
        )
        sums.append(jnp.dot(weights, piece[add_level], preferred_element_type=jnp.float32))
    projected = jnp.stack(sums).astype(jnp.bfloat16)
    col_weights = [
        weights_cols(
            offsets[direction, level, 1],
            ratio[direction, level, 0],
            ratio[direction, level, 1],
            pupil_cols,
            screen_cols,
            column_start,
            cols_dev,
        )
        for level in range(layers)
    ]
    total = jnp.zeros((pupil_rows // n_layer * lax.axis_size("layer"), pupil_cols), jnp.float32)
    for level in range(layers):
        total = total + jnp.dot(
            projected[level], col_weights[level], preferred_element_type=jnp.float32
        )
    phase = lax.psum_scatter(
        total.astype(jnp.bfloat16), "layer", scatter_dimension=0, tiled=True
    ).astype(jnp.float32)
    spots = imaging(phase, amplitude)[None]
    return (new_screens, spots)


def solution(mesh):
    return jax.shard_map(
        per_device,
        mesh=mesh,
        in_specs=(P(None, "dir", "layer"), P("layer", None), P(), P(), P()),
        out_specs=(P(None, "dir", "layer"), P("dir", "layer", None)),
        check_vma=False,
    )
```

profile of v0, /device:TPU:0, one launch (start us, length us, event | category | flops | bytes accessed | tf_op | source)
XLA Modules:
  0.0 353.2 jit_solution(13287869215477032080)
XLA Ops:
  8.6 2.1 collective-permute-start
  10.7 7.1 %collective-permute-start.1 = (bf16[3,512,8]{2,1,0:T(8,128)(2,1)S(1)}, bf16[3,512,8]{2,1,0:T(8,128)(2,1)S(1)}, u32[]{:S(2)}, u32[]{:S(2)}) collective-permute-start(bf16[3,512,8]{2,1,0:T(8,128)(2,1)S(1)} %get-tuple-element.8), channel_id=1, source_target_pairs={{4,0},{8,4},{12,8},{16,12},{20,16},{24,20},{28,24},{32,28},{36,32}... | collective-permute-start | bytes 73736 | tf_op jit(solution)/shard_map/ppermute | solution.py:19
  17.8 9.0 %collective-permute-done = bf16[3,512,8]{2,1,0:T(8,128)(2,1)S(1)} collective-permute-done((bf16[3,512,8]{2,1,0:T(8,128)(2,1)S(1)}, bf16[3,512,8]{2,1,0:T(8,128)(2,1)S(1)}, u32[]{:S(2)}, u32[]{:S(2)}) %collective-permute-start) | collective-permute-done | bytes 24608 | tf_op jit(solution)/shard_map/ppermute | solution.py:18
  27.0 1.7 collective-permute-start.3
  50.0 1.4 subtract_convert_fusion.3
  56.3 2.0 add_select_fusion.18
  58.4 2.0 add_select_fusion.22
  60.4 2.0 add_select_fusion.14
  62.4 2.1 add_select_fusion.6
  64.4 2.0 add_select_fusion.10
  66.5 2.0 add_select_fusion.2
  68.4 36.3 %all-gather.2.cloned.1.call-done = bf16[3,2048,512]{2,1,0:T(8,128)(2,1)} async-done(((bf16[3,512,512]{2,1,0:T(8,128)(2,1)}), bf16[3,2048,512]{2,1,0:T(8,128)(2,1)}) %all-gather.2.cloned.1.call-update) | async-done | bytes 6291472 | tf_op jit(solution)/shard_map/all_gather | solution.py:101
  104.7 8.1 %fusion.37 = f32[1024,1280]{1,0:T(8,128)} fusion(bf16[3,2048,512]{2,1,0:T(8,128)(2,1)} %all-gather.2.cloned.1.call-done, s32[1024]{0:T(1024)S(1)} %get-tuple-element.36, s32[1024]{0:T(1024)S(1)} %get-tuple-element.35, bf16[1024]{0:T(1024)(128)(2,1)S(1)} %get-tuple-element.40, bf16[1024]{0:T(1024)(128)(2,1)S(1)} %get-tuple-element.43, ...), kind=kOutput, calls=%fused_computation.45 | convolution fusion | flops 3501195264 | bytes 7369728 | tf_op jit(solution)/shard_map/dot_general | solution.py:128
  112.8 8.1 %fusion.40 = f32[1024,1280]{1,0:T(8,128)} fusion(bf16[3,2048,512]{2,1,0:T(8,128)(2,1)} %all-gather.2.cloned.1.call-done, s32[1024]{0:T(1024)S(1)} %get-tuple-element.38, s32[1024]{0:T(1024)S(1)} %get-tuple-element.37, bf16[1024]{0:T(1024)(128)(2,1)S(1)} %get-tuple-element.41, bf16[1024]{0:T(1024)(128)(2,1)S(1)} %get-tuple-element.44, ...), kind=kOutput, calls=%fused_computation.46 | convolution fusion | flops 3501195264 | bytes 7369728 | tf_op jit(solution)/shard_map/dot_general | solution.py:128
  120.9 9.2 %add_convert_fusion = bf16[1024,1280]{1,0:T(8,128)(2,1)} fusion(f32[1024,1280]{1,0:T(8,128)} %fusion.40, f32[1024,1280]{1,0:T(8,128)} %fusion.37, bf16[3,2048,512]{2,1,0:T(8,128)(2,1)} %all-gather.2.cloned.1.call-done, s32[1024]{0:T(1024)S(1)} %get-tuple-element.34, s32[1024]{0:T(1024)S(1)} %get-tuple-element.33, ...), kind=kOutput, calls=%fused_computation.12 | convolution fusion | flops 3505127424 | bytes 15234048 | tf_op jit(solution)/shard_map/dot_general | solution.py:128
  130.1 190.9 %reduce-scatter.2.cloned.1.call-done = bf16[32,1280]{1,0:T(8,128)(2,1)} async-done(((bf16[1024,1280]{1,0:T(8,128)(2,1)}), bf16[32,1280]{1,0:T(8,128)(2,1)}) %reduce-scatter.2.cloned.1.call-update) | async-done | bytes 81936 | tf_op jit(solution)/shard_map/reduce_scatter | solution.py:131
  321.0 1.5 fusion.73
  322.9 3.2 fusion.99
  326.1 3.2 fusion.95
  329.7 3.2 convolution_add_fusion.1
  334.2 3.2 convolution_subtract_fusion.1
  340.0 1.4 fusion.212
  342.6 1.9 copy.23
  344.5 1.8 broadcast_in_dim_reshape.3
  (41 shorter events, 18.2 us)
Async XLA Ops:
  7.2 19.7 %copy-start = (bf16[3,512,512]{2,1,0:T(8,128)(2,1)S(1)}, bf16[3,512,512]{2,1,0:T(8,128)(2,1)}, u32[]{:S(2)}) copy-start(bf16[3,512,512]{2,1,0:T(8,128)(2,1)} %param.5) | copy-start | bytes 4718596
  7.2 21.6 %copy-start.2 = (s32[3,2]{0,1:T(2,128)S(1)}, s32[3,2]{0,1:T(2,128)}, u32[]{:S(2)}) copy-start(s32[3,2]{0,1:T(2,128)} %param.7) | copy-start | bytes 76
  7.2 97.5 %all-gather.2.cloned.1.call-start = ((), (), s32[]{:S(2)}) async-start(), calls=%async_computation.1 | async-start | bytes 7864320 | tf_op jit(solution)/shard_map/all_gather | solution.py:101
  8.6 18.2 %collective-permute-start = (bf16[3,512,8]{2,1,0:T(8,128)(2,1)S(1)}, bf16[3,512,8]{2,1,0:T(8,128)(2,1)S(1)}, u32[]{:S(2)}, u32[]{:S(2)}) collective-permute-start(bf16[3,512,8]{2,1,0:T(8,128)(2,1)S(1)} %get-tuple-element.7), channel_id=1, source_target_pairs={{0,4},{4,8},{8,12},{12,16},{16,20},{20,24},{24,28},{28,32},{32,36}... | collective-permute-start | bytes 73736 | tf_op jit(solution)/shard_map/ppermute | solution.py:18
  10.7 16.1 %collective-permute-start.1 = (bf16[3,512,8]{2,1,0:T(8,128)(2,1)S(1)}, bf16[3,512,8]{2,1,0:T(8,128)(2,1)S(1)}, u32[]{:S(2)}, u32[]{:S(2)}) collective-permute-start(bf16[3,512,8]{2,1,0:T(8,128)(2,1)S(1)} %get-tuple-element.8), channel_id=1, source_target_pairs={{4,0},{8,4},{12,8},{16,12},{20,16},{24,20},{28,24},{32,28},{36,32}... | collective-permute-start | bytes 73736 | tf_op jit(solution)/shard_map/ppermute | solution.py:19
  27.0 10.1 %collective-permute-start.2 = (bf16[3,8,528]{2,1,0:T(8,128)(2,1)S(1)}, bf16[3,8,528]{2,1,0:T(8,128)(2,1)S(1)}, u32[]{:S(2)}, u32[]{:S(2)}) collective-permute-start(bf16[3,8,528]{2,1,0:T(8,128)(2,1)S(1)} %get-tuple-element.2), channel_id=1, source_target_pairs={{0,1},{1,2},{2,3},{3,0},{4,5},{5,6},{6,7},{7,4},{8,9},{9,10},{10,1... | collective-permute-start | bytes 76040 | tf_op jit(solution)/shard_map/ppermute | solution.py:18
  27.0 10.0 %collective-permute-start.3 = (bf16[3,8,528]{2,1,0:T(8,128)(2,1)S(1)}, bf16[3,8,528]{2,1,0:T(8,128)(2,1)S(1)}, u32[]{:S(2)}, u32[]{:S(2)}) collective-permute-start(bf16[3,8,528]{2,1,0:T(8,128)(2,1)S(1)} %get-tuple-element.3), channel_id=1, source_target_pairs={{1,0},{2,1},{3,2},{0,3},{5,4},{6,5},{7,6},{4,7},{9,8},{10,9},{11,1... | collective-permute-start | bytes 76040 | tf_op jit(solution)/shard_map/ppermute | solution.py:19
  39.3 1.6 copy-start.3
  39.3 10.0 %copy-start.4 = (s32[4,3,2]{0,2,1:T(2,128)S(1)}, s32[4,3,2]{0,2,1:T(2,128)}, u32[]{:S(2)}) copy-start(s32[4,3,2]{0,2,1:T(2,128)} %param.8) | copy-start | bytes 292
  40.7 280.3 %reduce-scatter.2.cloned.1.call-start = ((), (), s32[]{:S(2)}) async-start(), calls=%async_computation.2 | async-start | bytes 2703360 | tf_op jit(solution)/shard_map/reduce_scatter | solution.py:131
  130.1 190.9 %copy-start.1 = (f32[32,1280]{1,0:T(8,128)S(1)}, f32[32,1280]{1,0:T(8,128)}, u32[]{:S(2)}) copy-start(f32[32,1280]{1,0:T(8,128)} %param.6) | copy-start | bytes 491524
Sparse Core Ops, SparseCore 0:
  40.8 63.8 all-gather.1
  130.2 190.7 reduce-scatter.1
where the time goes:
time: 354 us; the launch traced here: 353 us
  waiting for transfers between devices  236 us (67%)
  matrix products  43.4 us (12%)
  between operations  29.6 us (8%)
  other arithmetic  23.6 us (7%)
  starting transfers between devices  11.2 us (3%)
  local copies, waits for them, and re-layouts  9.15 us (3%)
    reduce_scatter x1, waiting for transfers between devices, per_device(): lax.psum_scatter(total.astype(jnp.bfloat16), 'layer', scatter_dimension=0...  191 us
    all_gather x1, waiting for transfers between devices, per_device(): piece = lax.all_gather(new_screens, 'dir', axis=1, tiled=True)  36.3 us
    dot_general x3, matrix products, per_device(): jnp.dot(projected[level], col_weights[level], preferred_element_type=jnp....  25.4 us
    select_n x6, other arithmetic, spans(): upper = (base + 1) % length  12.1 us
    ppermute x2, waiting for transfers between devices, with_halo(): before = lax.ppermute(last, axis, up)  9.03 us
    ppermute x2, starting transfers between devices, with_halo(): after = lax.ppermute(initial, axis, down)  8.84 us
  transfers between devices with their start and end apart: 6, of which 3 were waited for; matrix products, arithmetic and copies ran while one was open for 6% of the time, Pallas kernels for 0%

commit v1 on v0

--- a/solution.py
+++ b/solution.py
@@ -98,7 +98,9 @@
         corner = (jnp.int32(WIND_MAX) - wind[level, 0], jnp.int32(WIND_MAX) - wind[level, 1])
         moved.append(lax.dynamic_slice(widened[level], corner, (rows_dev, cols_dev)))
     new_screens = jnp.stack(moved)
-    piece = lax.all_gather(new_screens, "dir", axis=1, tiled=True)
+    piece = jnp.concatenate(
+        lax.all_to_all(jnp.stack([new_screens] * lax.axis_size("dir")), "dir", 0, 0), axis=1
+    )
     sums = []
     for add_level in range(layers):
         weights = weights_rows(

time: 354 us -> 373 us (1.054)
  local copies, waits for them, and re-layouts: 9.15 us -> 18.9 us
  waiting for transfers between devices: 236 us -> 242 us
  starting transfers between devices: 11.2 us -> 16.6 us
    all_to_all x0 -> x1, waiting for transfers between devices: none -> 43.1 us  [per_device(): lax.all_to_all(jnp.stack([new_screens] * lax.axis_size('dir')), 'dir', 0, 0)]
    all_gather x1 -> x0, waiting for transfers between devices: 36.3 us -> none  [per_device(): piece = lax.all_gather(new_screens, 'dir', axis=1, tiled=True)]
    all_to_all x0 -> x1, starting transfers between devices: none -> 5.41 us  [per_device(): lax.all_to_all(jnp.stack([new_screens] * lax.axis_size('dir')), 'dir', 0, 0)]
    slice x0 -> x1, local copies, waits for them, and re-layouts: none -> 5.37 us  [per_device(): piece[add_level]]
where the time goes in v1:
time: 373 us; the launch traced here: 372 us
  waiting for transfers between devices  242 us (65%)
  matrix products  42.9 us (12%)
  between operations  29.1 us (8%)
  other arithmetic  22.8 us (6%)
  local copies, waits for them, and re-layouts  18.9 us (5%)
  starting transfers between devices  16.6 us (4%)
    reduce_scatter x1, waiting for transfers between devices, per_device(): lax.psum_scatter(total.astype(jnp.bfloat16), 'layer', scatter_dimension=0...  190 us
    all_to_all x1, waiting for transfers between devices, per_device(): lax.all_to_all(jnp.stack([new_screens] * lax.axis_size('dir')), 'dir', 0, 0)  43.1 us
    dot_general x3, matrix products, per_device(): jnp.dot(projected[level], col_weights[level], preferred_element_type=jnp....  24.9 us
    select_n x6, other arithmetic, spans(): upper = (base + 1) % length  12.1 us
    ppermute x2, waiting for transfers between devices, with_halo(): before = lax.ppermute(last, axis, up)  9.03 us
    ppermute x2, starting transfers between devices, with_halo(): after = lax.ppermute(initial, axis, down)  8.84 us
  transfers between devices with their start and end apart: 6, of which 3 were waited for; matrix products, arithmetic and copies ran while one was open for 6% of the time, Pallas kernels for 0%

profile of v1, /device:TPU:0, one launch (start us, length us, event | category | flops | bytes accessed | tf_op | source)
XLA Modules:
  0.0 372.2 jit_solution(1811025883237310558)
XLA Ops:
  8.6 2.1 collective-permute-start
  10.7 7.1 %collective-permute-start.1 = (bf16[3,512,8]{2,1,0:T(8,128)(2,1)S(1)}, bf16[3,512,8]{2,1,0:T(8,128)(2,1)S(1)}, u32[]{:S(2)}, u32[]{:S(2)}) collective-permute-start(bf16[3,512,8]{2,1,0:T(8,128)(2,1)S(1)} %get-tuple-element.11), channel_id=1, source_target_pairs={{4,0},{8,4},{12,8},{16,12},{20,16},{24,20},{28,24},{32,28},{36,32}... | collective-permute-start | bytes 73736 | tf_op jit(solution)/shard_map/ppermute | solution.py:19
  17.8 9.0 %collective-permute-done = bf16[3,512,8]{2,1,0:T(8,128)(2,1)S(1)} collective-permute-done((bf16[3,512,8]{2,1,0:T(8,128)(2,1)S(1)}, bf16[3,512,8]{2,1,0:T(8,128)(2,1)S(1)}, u32[]{:S(2)}, u32[]{:S(2)}) %collective-permute-start) | collective-permute-done | bytes 24608 | tf_op jit(solution)/shard_map/ppermute | solution.py:18
  27.0 1.7 collective-permute-start.3
  40.6 3.2 stack.9
  43.9 5.4 %all-to-all-start = ((bf16[4,3,512,512]{3,2,1,0:T(8,128)(2,1)}), bf16[4,3,512,512]{3,2,1,0:T(8,128)(2,1)}, u32[]{:S(2)}, u32[]{:S(2)}) async-start(bf16[4,3,512,512]{3,2,1,0:T(8,128)(2,1)} %stack.9), calls=%async_computation | async-start | bytes 12582912 | tf_op jit(solution)/shard_map/all_to_all | solution.py:102
  64.8 2.1 add_select_fusion.18
  66.8 1.9 add_select_fusion.22
  68.8 2.0 add_select_fusion.14
  70.7 2.1 add_select_fusion.6
  72.9 1.9 add_select_fusion.10
  74.8 2.0 add_select_fusion.2
  76.8 43.1 %all-to-all-done = bf16[4,3,512,512]{3,2,1,0:T(8,128)(2,1)} async-done(((bf16[4,3,512,512]{3,2,1,0:T(8,128)(2,1)}), bf16[4,3,512,512]{3,2,1,0:T(8,128)(2,1)}, u32[]{:S(2)}, u32[]{:S(2)}) %all-to-all-start) | async-done | bytes 6291488 | tf_op jit(solution)/shard_map/all_to_all | solution.py:102
  120.0 5.4 %fusion.209 = (bf16[1,4,512,512]{3,2,0,1:T(8,128)(2,1)S(1)}, bf16[1,4,512,512]{3,2,0,1:T(8,128)(2,1)}, bf16[1,4,512,512]{3,2,0,1:T(8,128)(2,1)}) fusion(bf16[3,4,512,512]{3,2,0,1:T(8,128)(2,1)} %bitcast.15), kind=kLoop, calls=%fused_computation.301 | loop fusion | bytes 12582912 | tf_op jit(solution)/shard_map/slice | solution.py:114
  125.4 8.1 %fusion.37 = f32[1024,1280]{1,0:T(8,128)} fusion(bf16[2048,512]{1,0:T(8,128)(2,1)} %bitcast.65, s32[1024]{0:T(1024)S(1)} %get-tuple-element.39, s32[1024]{0:T(1024)S(1)} %get-tuple-element.38, bf16[1024]{0:T(1024)(128)(2,1)S(1)} %get-tuple-element.43, bf16[1024]{0:T(1024)(128)(2,1)S(1)} %get-tuple-element.46, s32[1280]{0:T(1024)S(1)} %get-tuple-element.53, ...), kind=kOutput, calls=%fused_computation.42 | convolution fusion | flops 3501195264 | bytes 7369728 | tf_op jit(solution)/shard_map/dot_general | solution.py:130
  133.5 8.2 %fusion.40 = f32[1024,1280]{1,0:T(8,128)} fusion(bf16[2048,512]{1,0:T(8,128)(2,1)} %bitcast.64, s32[1024]{0:T(1024)S(1)} %get-tuple-element.41, s32[1024]{0:T(1024)S(1)} %get-tuple-element.40, bf16[1024]{0:T(1024)(128)(2,1)S(1)} %get-tuple-element.44, bf16[1024]{0:T(1024)(128)(2,1)S(1)} %get-tuple-element.47, s32[1280]{0:T(1024)S(1)} %get-tuple-element.49, ...), kind=kOutput, calls=%fused_computation.43 | convolution fusion | flops 3501195264 | bytes 7369728 | tf_op jit(solution)/shard_map/dot_general | solution.py:130
  141.7 8.6 %add_convert_fusion = bf16[1024,1280]{1,0:T(8,128)(2,1)} fusion(f32[1024,1280]{1,0:T(8,128)} %fusion.40, f32[1024,1280]{1,0:T(8,128)} %fusion.37, s32[1280]{0:T(1024)S(1)} %get-tuple-element.57, s32[1280]{0:T(1024)S(1)} %get-tuple-element.56, s32[512]{0:T(512)S(1)} %iota_add_fusion, bf16[2048,512]{1,0:T(8,128)(2,1)S(1)} %bitcast.63, ...), kind=kOutput, calls=%fused_computation.12 | convolution fusion | flops 3505127424 | bytes 15234048 | tf_op jit(solution)/shard_map/dot_general | solution.py:130
  150.3 189.8 %reduce-scatter.2.cloned.1.call-done = bf16[32,1280]{1,0:T(8,128)(2,1)} async-done(((bf16[1024,1280]{1,0:T(8,128)(2,1)}), bf16[32,1280]{1,0:T(8,128)(2,1)}) %reduce-scatter.2.cloned.1.call-update) | async-done | bytes 81936 | tf_op jit(solution)/shard_map/reduce_scatter | solution.py:133
  342.0 3.2 fusion.99
  345.2 3.2 fusion.95
  348.8 3.2 convolution_add_fusion.1
  353.3 3.2 convolution_subtract_fusion.1
  361.6 1.9 copy.23
  363.6 1.8 broadcast_in_dim_reshape.3
  (44 shorter events, 22.8 us)
Async XLA Ops:
  7.2 19.7 %copy-start = (bf16[3,512,512]{2,1,0:T(8,128)(2,1)S(1)}, bf16[3,512,512]{2,1,0:T(8,128)(2,1)}, u32[]{:S(2)}) copy-start(bf16[3,512,512]{2,1,0:T(8,128)(2,1)} %param.5) | copy-start | bytes 4718596
  7.2 21.6 %copy-start.3 = (s32[3,2]{0,1:T(2,128)S(1)}, s32[3,2]{0,1:T(2,128)}, u32[]{:S(2)}) copy-start(s32[3,2]{0,1:T(2,128)} %param.7) | copy-start | bytes 76
  8.6 18.2 %collective-permute-start = (bf16[3,512,8]{2,1,0:T(8,128)(2,1)S(1)}, bf16[3,512,8]{2,1,0:T(8,128)(2,1)S(1)}, u32[]{:S(2)}, u32[]{:S(2)}) collective-permute-start(bf16[3,512,8]{2,1,0:T(8,128)(2,1)S(1)} %get-tuple-element.10), channel_id=1, source_target_pairs={{0,4},{4,8},{8,12},{12,16},{16,20},{20,24},{24,28},{28,32},{32,36}... | collective-permute-start | bytes 73736 | tf_op jit(solution)/shard_map/ppermute | solution.py:18
  10.7 16.1 %collective-permute-start.1 = (bf16[3,512,8]{2,1,0:T(8,128)(2,1)S(1)}, bf16[3,512,8]{2,1,0:T(8,128)(2,1)S(1)}, u32[]{:S(2)}, u32[]{:S(2)}) collective-permute-start(bf16[3,512,8]{2,1,0:T(8,128)(2,1)S(1)} %get-tuple-element.11), channel_id=1, source_target_pairs={{4,0},{8,4},{12,8},{16,12},{20,16},{24,20},{28,24},{32,28},{36,32}... | collective-permute-start | bytes 73736 | tf_op jit(solution)/shard_map/ppermute | solution.py:19
  26.9 10.1 %collective-permute-start.2 = (bf16[3,8,528]{2,1,0:T(8,128)(2,1)S(1)}, bf16[3,8,528]{2,1,0:T(8,128)(2,1)S(1)}, u32[]{:S(2)}, u32[]{:S(2)}) collective-permute-start(bf16[3,8,528]{2,1,0:T(8,128)(2,1)S(1)} %get-tuple-element.5), channel_id=1, source_target_pairs={{0,1},{1,2},{2,3},{3,0},{4,5},{5,6},{6,7},{7,4},{8,9},{9,10},{10,1... | collective-permute-start | bytes 76040 | tf_op jit(solution)/shard_map/ppermute | solution.py:18
  27.0 10.0 %collective-permute-start.3 = (bf16[3,8,528]{2,1,0:T(8,128)(2,1)S(1)}, bf16[3,8,528]{2,1,0:T(8,128)(2,1)S(1)}, u32[]{:S(2)}, u32[]{:S(2)}) collective-permute-start(bf16[3,8,528]{2,1,0:T(8,128)(2,1)S(1)} %get-tuple-element.6), channel_id=1, source_target_pairs={{1,0},{2,1},{3,2},{0,3},{5,4},{6,5},{7,6},{4,7},{9,8},{10,9},{11,1... | collective-permute-start | bytes 76040 | tf_op jit(solution)/shard_map/ppermute | solution.py:19
  39.5 1.1 copy-start.1
  43.9 5.7 %copy-start.4 = (s32[4,3,2]{0,2,1:T(2,128)S(1)}, s32[4,3,2]{0,2,1:T(2,128)}, u32[]{:S(2)}) copy-start(s32[4,3,2]{0,2,1:T(2,128)} %param.9) | copy-start | bytes 292
  43.9 13.6 %copy-start.5 = (s32[4,3,2]{0,2,1:T(2,128)S(1)}, s32[4,3,2]{0,2,1:T(2,128)}, u32[]{:S(2)}) copy-start(s32[4,3,2]{0,2,1:T(2,128)} %param.8) | copy-start | bytes 292
  43.9 76.1 %all-to-all-start = ((bf16[4,3,512,512]{3,2,1,0:T(8,128)(2,1)}), bf16[4,3,512,512]{3,2,1,0:T(8,128)(2,1)}, u32[]{:S(2)}, u32[]{:S(2)}) async-start(bf16[4,3,512,512]{3,2,1,0:T(8,128)(2,1)} %stack.9), calls=%async_computation | async-start | bytes 12582912 | tf_op jit(solution)/shard_map/all_to_all | solution.py:102
  49.3 290.8 %reduce-scatter.2.cloned.1.call-start = ((), (), s32[]{:S(2)}) async-start(), calls=%async_computation.2 | async-start | bytes 2703360 | tf_op jit(solution)/shard_map/reduce_scatter | solution.py:133
  150.3 189.8 %copy-start.2 = (f32[32,1280]{1,0:T(8,128)S(1)}, f32[32,1280]{1,0:T(8,128)}, u32[]{:S(2)}) copy-start(f32[32,1280]{1,0:T(8,128)} %param.6) | copy-start | bytes 491524
Sparse Core Ops, SparseCore 0:
  150.4 189.6 reduce-scatter.1
